TPU v7x, 32 devices: a whole 2x2x4 slice. The times are simulated.
32 devices in a mesh: row: 4 (over y, x), col: 8 (over z, core).
Axes of the slice: x: 2, y: 2, z: 4, core: 2. Of those that a mesh axis runs over, the one named last changes fastest.
Arguments:
- velocities: bfloat16 [1024, 30720], P(None, 'row'), may hold values from -60 to 60, as said below
- modes_panel: bfloat16 [30720, 4096], P('row', 'col'), may hold values from -1 to 1
- atom_slot: int32 [10240], P('row'), may hold values from 0 to 2559, as said below
- lag_offsets: int32 [8], replicated, may hold values from 0 to 256, as said below
Outputs:
- correlations: float32 [8, 4096, 4096], P(None, 'row', 'col')
Inputs may be any that keep to these rules, and one draw needn't show every extreme that they name: `velocities`: every snapshot row has its own scale. Within each aligned block of 2560 atoms, atom_slot is a permutation of 0 to 2559. `lag_offsets`: one of the lags equals 256.
All inputs are finite; a program needn't handle non-finite values.
Results may differ from a plain program's by a relative error of at most 0.0041.
Values may be sent and summed in bfloat16 or wider, within the bound.
No kernel may reach another device: no remote copies, remote signals or barrier semaphores. Data moves between devices by JAX's collectives and lax.ppermute only.
A program may use at most 128 MiB of HBM per device.

v0:
```python
import jax
import jax.numpy as jnp
from jax import lax
from jax.sharding import PartitionSpec as P

M = 4096
LAGS = 8
MAXLAG = 256
epsilon = 1e-06


def from_root(block, axis, owner):
    block = jnp.where(lax.axis_index(axis) == owner, block, jnp.zeros_like(block))
    return lax.psum(block, axis)


def reorder(modes_panel, atom_slot):
    per_atom = modes_panel.reshape(atom_slot.shape[0], 3, modes_panel.shape[1])
    return jnp.take(per_atom, atom_slot, axis=0).reshape(modes_panel.shape)


def correlate(row_modes, column_modes, lag_offsets):
    snapshots = column_modes.shape[0]
    padded = jnp.concatenate(
        [column_modes, jnp.zeros((MAXLAG, column_modes.shape[1]), jnp.bfloat16)], axis=0
    )
    results = []
    for number in range(LAGS):
        offset = lag_offsets[number]
        shifted = lax.dynamic_slice_in_dim(padded, offset, snapshots, 0)
        product = lax.dot_general(
            row_modes, shifted, (((0,), (0,)), ((), ())), preferred_element_type=jnp.float32
        )
        results.append(product * lax.rsqrt((snapshots - offset).astype(jnp.float32)))
    return jnp.stack(results)


def local(velocities, modes_panel, atom_slot, lag_offsets):
    panel = reorder(modes_panel, atom_slot)
    row_count = lax.axis_size("row")
    col_count = lax.axis_size("col")
    partial_terms = jnp.dot(velocities, panel, preferred_element_type=jnp.float32)
    projected = lax.psum(partial_terms, "row")
    energy = lax.psum(jnp.sum(projected * projected, axis=1), "col")
    column_modes = (projected * lax.rsqrt(energy / M + epsilon)[:, None]).astype(jnp.bfloat16)
    owners = col_count // row_count
    pieces = [
        from_root(column_modes, "col", lax.axis_index("row") * owners + owner)
        for owner in range(owners)
    ]
    row_modes = jnp.concatenate(pieces, axis=1)
    return correlate(row_modes, column_modes, lag_offsets)


def solution(mesh):
    return jax.shard_map(
        local,
        mesh=mesh,
        in_specs=(P(None, "row"), P("row", "col"), P("row"), P()),
        out_specs=P(None, "row", "col"),
        check_vma=False,
    )
```

profile of v0, /device:TPU:0, one launch (start us, length us, event | category | flops | bytes accessed | tf_op | source)
XLA Modules:
  0.0 267.6 jit_solution(14538257471376262001)
XLA Ops:
  6.5 0.0 all-reduce.5.cloned.1.call-start
  6.5 0.7 compare_select_fusion
  7.2 0.7 compare_and_fusion
  8.0 20.7 %reshape.12 = bf16[2560,3,512]{2,1,0:T(4,128)(2,1)} reshape(bf16[7680,512]{1,0:T(8,128)(2,1)} %param.5) | data formatting | bytes 15728640 | tf_op jit(solution)/shard_map/reshape | solution.py:18
  28.7 17.1 %gather_fusion = bf16[2560,3,512]{2,1,0:T(4,128)(2,1)} fusion(bf16[2560,3,512]{2,1,0:T(4,128)(2,1)} %reshape.12, s32[3072]{0:T(1024)S(1)} %pad_clamp_fusion), kind=kCustom, calls=%fused_computation | custom fusion | bytes 15738880 | tf_op jit(solution)/shard_map/jit(_take)/gather | solution.py:19
  45.9 20.0 %gather.7 = bf16[7680,512]{1,0:T(8,128)(2,1)} reshape(bf16[2560,3,512]{2,1,0:T(4,128)(2,1)} %gather_fusion) | data formatting | bytes 15728640 | tf_op jit(solution)/shard_map/jit(_take)/gather | solution.py:19
  65.9 1.3 broadcast_in_dim.18
  67.2 1.1 broadcast_in_dim.19
  68.3 16.5 %fusion.4 = f32[1024,512]{0,1:T(8,128)} fusion(bf16[1024,7680]{1,0:T(8,128)(2,1)} %param.4, bf16[7680,512]{1,0:T(8,128)(2,1)} %gather.7, pred[7680]{0:T(1024)(128)(4,1)S(1)} %broadcast_in_dim.19), kind=kOutput, calls=%fused_computation.15 | convolution fusion | flops 8056995840 | bytes 25697792 | tf_op jit(solution)/shard_map/dot_general | solution.py:42
  84.8 0.0 all-reduce.5.cloned.1.call-update
  84.9 0.0 all-reduce.7.cloned.1.call-start
  84.9 72.3 %all-reduce.5.cloned.1.call-done = f32[1024,512]{0,1:T(8,128)} async-done(((f32[1024,512]{0,1:T(8,128)}), f32[1024,512]{0,1:T(8,128)}) %all-reduce.5.cloned.1.call-update) | async-done | bytes 2097168 | tf_op jit(solution)/shard_map/psum | solution.py:43
  157.2 0.0 copy-start
  157.2 1.9 multiply_reduce_fusion
  159.1 16.4 %psum.29 = f32[1024]{0:T(1024)S(1)} all-reduce(f32[1024]{0:T(1024)S(1)} %multiply_reduce_fusion), channel_id=1, replica_groups=mesh['row'=4,'col'=8] {'col'}, use_global_device_ids=true, to_apply=%region_2.3 | all-reduce | flops 1024 | bytes 8192 | tf_op jit(solution)/shard_map/psum | solution.py:44
  175.5 0.0 copy-done
  175.5 1.4 broadcast_select_fusion
  176.9 0.0 copy-start.2
  176.9 1.1 broadcast_select_fusion.1
  178.0 0.0 all-reduce.7.cloned.1.call-update
  178.0 0.0 copy-done.2
  178.0 0.7 fusion.24
  198.4 42.2 %all-reduce.7.cloned.1.call-done = (bf16[1024,512]{0,1:T(8,128)(2,1)}, bf16[1024,512]{0,1:T(8,128)(2,1)}) async-done(((bf16[1024,512]{0,1:T(8,128)(2,1)}, bf16[1024,512]{0,1:T(8,128)(2,1)}), (bf16[1024,512]{0,1:T(8,128)(2,1)}, bf16[1024,512]{0,1:T(8,128)(2,1)})) %all-reduce.7.cloned.1.call-update) | async-done | bytes 2097168 | tf_op jit(solution)/shard_map/psum | solution.py:14
  240.6 0.0 copy-start.1
  240.6 1.4 constant_dynamic-update-slice_fusion.1
  242.0 0.2 copy-done.1
  242.2 0.1 constant_dynamic-update-slice_fusion
  242.2 1.4 bitcast_dynamic-update-slice_fusion.7
  243.6 1.4 bitcast_dynamic-update-slice_fusion.6
  245.0 1.4 bitcast_dynamic-update-slice_fusion.5
  246.4 1.4 bitcast_dynamic-update-slice_fusion.4
  247.8 1.4 bitcast_dynamic-update-slice_fusion.3
  249.1 1.4 bitcast_dynamic-update-slice_fusion.2
  250.5 1.4 bitcast_dynamic-update-slice_fusion.1
  251.9 0.0 copy-start.3
  251.9 6.2 %copy-done.3 = f32[8,1024,512]{2,1,0:T(8,128)} copy-done((f32[8,1024,512]{2,1,0:T(8,128)}, f32[8,1024,512]{2,1,0:T(8,128)S(1)}, u32[]{:S(2)}) %copy-start.3) | copy-done | bytes 16777240
  258.1 2.7 %bitcast_dynamic-update-slice_fusion = f32[8,1024,512]{2,1,0:T(8,128)} fusion(f32[8,1024,512]{2,1,0:T(8,128)} %copy-done.3, bf16[1024,1024]{0,1:T(8,128)(2,1)S(1)} %constant_dynamic-update-slice_fusion, s32[]{:T(128)S(6)} %select_n.61, bf16[1024,512]{0,1:T(8,128)(2,1)S(1)} %get-tuple-element.8, f32[]{:T(128)S(6)} %rsqrt.35), kind=kOutput, calls=%fused_computation.5 | convolution fusion | flops 1074266112 | bytes 5242888 | tf_op jit(solution)/shard_map/dot_general | solution.py:31
  (2 shorter events, 0.0 us)
Async XLA Ops:
  6.5 150.7 %all-reduce.5.cloned.1.call-start = ((), (), s32[]{:S(2)}) async-start(), calls=%async_computation | async-start | bytes 4194304 | tf_op jit(solution)/shard_map/psum | solution.py:43
  84.9 155.8 %all-reduce.7.cloned.1.call-start = ((), (), s32[]{:S(2)}) async-start(), calls=%async_computation.1 | async-start | bytes 4194304 | tf_op jit(solution)/shard_map/psum | solution.py:14
  157.2 18.3 %copy-start = (f32[1024,512]{0,1:T(8,128)S(1)}, f32[1024,512]{0,1:T(8,128)}, u32[]{:S(2)}) copy-start(f32[1024,512]{0,1:T(8,128)} %all-reduce.5.cloned.1.call-done) | copy-start | bytes 6291460
  176.9 1.1 copy-start.2
  240.6 1.5 copy-start.1
  251.9 6.2 %copy-start.3 = (f32[8,1024,512]{2,1,0:T(8,128)}, f32[8,1024,512]{2,1,0:T(8,128)S(1)}, u32[]{:S(2)}) copy-start(f32[8,1024,512]{2,1,0:T(8,128)S(1)} %bitcast_dynamic-update-slice_fusion.1) | copy-start | bytes 50331652
Sparse Core Ops, SparseCore 0:
  85.0 72.1 all-reduce.4
  178.1 62.4 all-reduce.6
where the time goes:
time: 269 us; the launch traced here: 268 us
  waiting for transfers between devices  115 us (43%)
  local copies, waits for them, and re-layouts  68.8 us (26%)
  between operations  33.2 us (12%)
  matrix products  28.9 us (11%)
  blocking collectives  16.4 us (6%)
  other arithmetic  5.85 us (2%)
    psum x1, waiting for transfers between devices, local(): projected = lax.psum(partial_terms, 'row')  72.3 us
    psum x1, waiting for transfers between devices, from_root(): return lax.psum(block, axis)  42.2 us
    gather x2, local copies, waits for them, and re-layouts, reorder(): return jnp.take(per_atom, atom_slot, axis=0).reshape(modes_panel.shape)  37.2 us
    reshape x1, local copies, waits for them, and re-layouts, reorder(): per_atom = modes_panel.reshape(atom_slot.shape[0], 3, modes_panel.shape[1])  20.7 us
    dot_general x1, matrix products, local(): jnp.dot(velocities, panel, preferred_element_type=jnp.float32)  16.5 us
    psum x1, blocking collectives, local(): energy = lax.psum(jnp.sum(projected * projected, axis=1), 'col')  16.4 us
    dot_general x8, matrix products, correlate(): lax.dot_general(row_modes, shifted, (((0,), (0,)), ((), ())), preferred_e...  12.3 us
    unnamed x9, local copies, waits for them, and re-layouts  7.7 us
  transfers between devices with their start and end apart: 2, of which 2 were waited for; matrix products, arithmetic and copies ran while one was open for 0% of the time, Pallas kernels for 0%

commit v1 on v0

--- a/solution.py
+++ b/solution.py
@@ -40,7 +40,11 @@
     row_count = lax.axis_size("row")
     col_count = lax.axis_size("col")
     partial_terms = jnp.dot(velocities, panel, preferred_element_type=jnp.float32)
-    projected = lax.psum(partial_terms, "row")
+    projected = partial_terms
+    for hop in (1, 2):
+        projected = projected + lax.ppermute(
+            projected, "row", [(dev, dev ^ hop) for dev in range(4)]
+        )
     energy = lax.psum(jnp.sum(projected * projected, axis=1), "col")
     column_modes = (projected * lax.rsqrt(energy / M + epsilon)[:, None]).astype(jnp.bfloat16)
     owners = col_count // row_count

time: 269 us -> 294 us (1.093)
  waiting for transfers between devices: 115 us -> 134 us
  starting transfers between devices: 0.04 us -> 4.87 us
  other arithmetic: 5.85 us -> 9.27 us
    ppermute x0 -> x2, waiting for transfers between devices: none -> 90.8 us  [local(): lax.ppermute(projected, 'row', [(dev, dev ^ hop) for dev in range(4)])]
    psum x1 -> x0, waiting for transfers between devices: 72.3 us -> none  [local(): projected = lax.psum(partial_terms, 'row')]
    ppermute x0 -> x2, starting transfers between devices: none -> 4.86 us  [local(): lax.ppermute(projected, 'row', [(dev, dev ^ hop) for dev in range(4)])]
    unnamed x9 -> x7, local copies, waits for them, and re-layouts: 7.7 us -> 7.7 us
  transfers between devices with their start and end apart: 2 -> 3, of which waited for: 2 -> 3; matrix products, arithmetic and copies ran while one was open for 0% -> 0% of each run, Pallas kernels for 0% -> 0%
where the time goes in v1:
time: 294 us; the launch traced here: 293 us
  waiting for transfers between devices  134 us (46%)
  local copies, waits for them, and re-layouts  68.7 us (23%)
  between operations  33.5 us (11%)
  matrix products  27.7 us (9%)
  blocking collectives  15 us (5%)
  other arithmetic  9.27 us (3%)
  starting transfers between devices  4.87 us (2%)
    ppermute x2, waiting for transfers between devices, local(): lax.ppermute(projected, 'row', [(dev, dev ^ hop) for dev in range(4)])  90.8 us
    psum x1, waiting for transfers between devices, from_root(): return lax.psum(block, axis)  43 us
    gather x2, local copies, waits for them, and re-layouts, reorder(): return jnp.take(per_atom, atom_slot, axis=0).reshape(modes_panel.shape)  37.2 us
    reshape x1, local copies, waits for them, and re-layouts, reorder(): per_atom = modes_panel.reshape(atom_slot.shape[0], 3, modes_panel.shape[1])  20.7 us
    dot_general x1, matrix products, local(): jnp.dot(velocities, panel, preferred_element_type=jnp.float32)  15.3 us
    psum x1, blocking collectives, local(): energy = lax.psum(jnp.sum(projected * projected, axis=1), 'col')  15 us
    dot_general x8, matrix products, correlate(): lax.dot_general(row_modes, shifted, (((0,), (0,)), ((), ())), preferred_e...  12.3 us
    unnamed x7, local copies, waits for them, and re-layouts  7.7 us
  transfers between devices with their start and end apart: 3, of which 3 were waited for; matrix products, arithmetic and copies ran while one was open for 0% of the time, Pallas kernels for 0%

profile of v1, /device:TPU:0, one launch (start us, length us, event | category | flops | bytes accessed | tf_op | source)
XLA Modules:
  0.0 292.8 jit_solution(14202692663391169260)
XLA Ops:
  6.5 0.0 all-reduce.4.cloned.1.call-start
  6.5 0.7 compare_select_fusion
  7.2 0.7 compare_and_fusion
  8.0 20.7 %reshape.12 = bf16[2560,3,512]{2,1,0:T(4,128)(2,1)} reshape(bf16[7680,512]{1,0:T(8,128)(2,1)} %param.5) | data formatting | bytes 15728640 | tf_op jit(solution)/shard_map/reshape | solution.py:18
  28.7 17.1 %gather_fusion = bf16[2560,3,512]{2,1,0:T(4,128)(2,1)} fusion(bf16[2560,3,512]{2,1,0:T(4,128)(2,1)} %reshape.12, s32[3072]{0:T(1024)S(1)} %pad_clamp_fusion), kind=kCustom, calls=%fused_computation | custom fusion | bytes 15738880 | tf_op jit(solution)/shard_map/jit(_take)/gather | solution.py:19
  45.8 20.0 %gather.7 = bf16[7680,512]{1,0:T(8,128)(2,1)} reshape(bf16[2560,3,512]{2,1,0:T(4,128)(2,1)} %gather_fusion) | data formatting | bytes 15728640 | tf_op jit(solution)/shard_map/jit(_take)/gather | solution.py:19
  65.9 1.3 broadcast_in_dim.18
  67.2 1.1 broadcast_in_dim.19
  68.3 15.3 %fusion.4 = f32[1024,512]{0,1:T(8,128)S(1)} fusion(bf16[1024,7680]{1,0:T(8,128)(2,1)} %param.4, bf16[7680,512]{1,0:T(8,128)(2,1)} %gather.7, pred[7680]{0:T(1024)(128)(4,1)S(1)} %broadcast_in_dim.19), kind=kOutput, calls=%fused_computation.15 | convolution fusion | flops 8056995840 | bytes 25697792 | tf_op jit(solution)/shard_map/dot_general | solution.py:42
  83.6 3.0 %collective-permute-start = (f32[1024,512]{0,1:T(8,128)S(1)}, f32[1024,512]{0,1:T(8,128)S(1)}, u32[]{:S(2)}, u32[]{:S(2)}) collective-permute-start(f32[1024,512]{0,1:T(8,128)S(1)} %fusion.4), channel_id=1, source_target_pairs={{0,8},{8,0},{16,24},{24,16},{1,9},{9,1},{17,25},{25,17},{2,10},{10... | collective-permute-start | bytes 6291464 | tf_op jit(solution)/shard_map/ppermute | solution.py:45
  86.6 45.6 %collective-permute-done = f32[1024,512]{0,1:T(8,128)S(1)} collective-permute-done((f32[1024,512]{0,1:T(8,128)S(1)}, f32[1024,512]{0,1:T(8,128)S(1)}, u32[]{:S(2)}, u32[]{:S(2)}) %collective-permute-start) | collective-permute-done | bytes 2097184 | tf_op jit(solution)/shard_map/ppermute | solution.py:45
  132.3 0.4 add.57
  132.7 1.8 collective-permute-start.1
  134.5 45.1 %collective-permute-done.1 = f32[1024,512]{0,1:T(8,128)} collective-permute-done((f32[1024,512]{0,1:T(8,128)S(1)}, f32[1024,512]{0,1:T(8,128)}, u32[]{:S(2)}, u32[]{:S(2)}) %collective-permute-start.1) | collective-permute-done | bytes 2097184 | tf_op jit(solution)/shard_map/ppermute | solution.py:45
  179.6 3.4 %multiply_reduce_fusion = (f32[1024]{0:T(1024)S(1)}, f32[1024,512]{0,1:T(8,128)}) fusion(f32[1024,512]{0,1:T(8,128)S(1)} %add.57, f32[1024,512]{0,1:T(8,128)} %collective-permute-done.1), kind=kLoop, calls=%fused_computation.14 | loop fusion | flops 1571840 | bytes 6295552 | tf_op jit(solution)/shard_map/reduce_sum | solution.py:48
  183.0 15.0 %psum.21 = f32[1024]{0:T(1024)S(1)} all-reduce(f32[1024]{0:T(1024)S(1)} %get-tuple-element.9), channel_id=1, replica_groups=mesh['row'=4,'col'=8] {'col'}, use_global_device_ids=true, to_apply=%region_1.2 | all-reduce | flops 1024 | bytes 8192 | tf_op jit(solution)/shard_map/psum | solution.py:48
  198.1 3.0 %broadcast_select_fusion = (bf16[1024,512]{0,1:T(8,128)(2,1)}, bf16[1024,512]{0,1:T(8,128)(2,1)S(1)}) fusion(pred[]{:T(512)S(6)} %eq.7, f32[1024,512]{0,1:T(8,128)} %get-tuple-element.10, f32[1024]{0:T(1024)S(1)} %add_rsqrt_fusion), kind=kLoop, calls=%fused_computation.24 | loop fusion | flops 1572864 | bytes 4198401 | tf_op jit(solution)/shard_map/jit(_where)/select_n | solution.py:13
  201.1 0.0 copy-start.1
  201.1 1.0 broadcast_select_fusion.1
  202.1 0.0 all-reduce.4.cloned.1.call-update
  202.2 0.0 copy-done.1
  202.2 0.7 fusion.24
  222.8 43.0 %all-reduce.4.cloned.1.call-done = (bf16[1024,512]{0,1:T(8,128)(2,1)}, bf16[1024,512]{0,1:T(8,128)(2,1)}) async-done(((bf16[1024,512]{0,1:T(8,128)(2,1)}, bf16[1024,512]{0,1:T(8,128)(2,1)}), (bf16[1024,512]{0,1:T(8,128)(2,1)}, bf16[1024,512]{0,1:T(8,128)(2,1)})) %all-reduce.4.cloned.1.call-update) | async-done | bytes 2097168 | tf_op jit(solution)/shard_map/psum | solution.py:14
  265.8 0.0 copy-start
  265.8 1.4 constant_dynamic-update-slice_fusion.1
  267.2 0.2 copy-done
  267.3 0.1 constant_dynamic-update-slice_fusion
  267.4 1.4 bitcast_dynamic-update-slice_fusion.7
  268.8 1.4 bitcast_dynamic-update-slice_fusion.6
  270.2 1.4 bitcast_dynamic-update-slice_fusion.5
  271.5 1.4 bitcast_dynamic-update-slice_fusion.4
  272.9 1.4 bitcast_dynamic-update-slice_fusion.3
  274.3 1.4 bitcast_dynamic-update-slice_fusion.2
  275.7 1.4 bitcast_dynamic-update-slice_fusion.1
  277.1 0.0 copy-start.2
  277.1 6.2 %copy-done.2 = f32[8,1024,512]{2,1,0:T(8,128)} copy-done((f32[8,1024,512]{2,1,0:T(8,128)}, f32[8,1024,512]{2,1,0:T(8,128)S(1)}, u32[]{:S(2)}) %copy-start.2) | copy-done | bytes 16777240
  283.2 2.7 bitcast_dynamic-update-slice_fusion
  (2 shorter events, 0.0 us)
Async XLA Ops:
  6.5 259.2 %all-reduce.4.cloned.1.call-start = ((), (), s32[]{:S(2)}) async-start(), calls=%async_computation | async-start | bytes 4194304 | tf_op jit(solution)/shard_map/psum | solution.py:14
  83.6 48.7 %collective-permute-start = (f32[1024,512]{0,1:T(8,128)S(1)}, f32[1024,512]{0,1:T(8,128)S(1)}, u32[]{:S(2)}, u32[]{:S(2)}) collective-permute-start(f32[1024,512]{0,1:T(8,128)S(1)} %fusion.4), channel_id=1, source_target_pairs={{0,8},{8,0},{16,24},{24,16},{1,9},{9,1},{17,25},{25,17},{2,10},{10... | collective-permute-start | bytes 6291464 | tf_op jit(solution)/shard_map/ppermute | solution.py:45
  132.7 47.0 %collective-permute-start.1 = (f32[1024,512]{0,1:T(8,128)S(1)}, f32[1024,512]{0,1:T(8,128)}, u32[]{:S(2)}, u32[]{:S(2)}) collective-permute-start(f32[1024,512]{0,1:T(8,128)S(1)} %add.57), channel_id=1, source_target_pairs={{0,16},{8,24},{16,0},{24,8},{1,17},{9,25},{17,1},{25,9},{2,18},{10... | collective-permute-start | bytes 6291464 | tf_op jit(solution)/shard_map/ppermute | solution.py:45
  201.1 1.1 copy-start.1
  265.8 1.5 copy-start
  277.1 6.2 %copy-start.2 = (f32[8,1024,512]{2,1,0:T(8,128)}, f32[8,1024,512]{2,1,0:T(8,128)S(1)}, u32[]{:S(2)}) copy-start(f32[8,1024,512]{2,1,0:T(8,128)S(1)} %bitcast_dynamic-update-slice_fusion.1) | copy-start | bytes 50331652
Sparse Core Ops, SparseCore 0:
  202.3 63.4 all-reduce.3
